TPU v7x, 32 devices: a whole 2x2x4 slice. The times are simulated.
32 devices in a mesh: clus: 8 (over z, core), lvl: 4 (over y, x).
Axes of the slice: x: 2, y: 2, z: 4, core: 2. Of those that a mesh axis runs over, the one named last changes fastest.
Arguments:
- krylov_basis: float32 [8, 4, 2048], P(None, 'lvl', 'clus'), may hold values from -90 to 90
- near_block: bfloat16 [4, 8, 4, 256, 256], P('lvl', 'clus'), may hold values from -1 to 2.5
- near_col: int32 [4, 8, 4], P('lvl', 'clus'), may hold values from 0 to 7, as said below
- near_count: int32 [4, 8], P('lvl', 'clus'), may hold values from 1 to 4, as said below
- far_col: int32 [4, 8, 6], P('lvl', 'clus'), may hold values from 0 to 7, as said below
- v_basis: bfloat16 [4, 8, 32, 256], P('lvl', 'clus'), may hold values from -0.375 to 0.375
- u_basis: bfloat16 [4, 8, 32, 256], P('lvl', 'clus'), may hold values from -1 to 1
- far_coupling: float32 [4, 8, 6, 32, 32], P('lvl', 'clus'), may hold values from -0.4375 to 0.4375
- transfer: float32 [4, 8, 32, 32], P('lvl', 'clus'), may hold values from -1 to 1
- top_coupling: float32 [4, 8, 4, 32, 32], P('lvl', 'clus'), may hold values from -0.5 to 0.5
Outputs:
- q_next: float32 [4, 4, 2048], P(None, 'lvl', 'clus')
- coeffs: float32 [2, 12, 4], replicated
Inputs may be any that keep to these rules, and one draw needn't show every extreme that they name: `near_col`: slot 0 of every leaf names the leaf itself; every other slot names leaf i - 1 or leaf i + 1 of the same subtree. Slots at or beyond the leaf's near_count name such leaves too, and their blocks are ignored. `near_count`: in some aligned run of 1 leaves every leaf has 4. `far_col`: A partner lies in the same subtree, in an aligned run of 1 leaves other than the leaf's own. Slot 0 names a leaf of the run just before the leaf's own, runs counted cyclically within the subtree.
All inputs are finite; a program needn't handle non-finite values.
Results may differ from a plain program's by a relative error of at most 0.00037.
Values may be sent and summed in bfloat16 or wider, within the bound.
No kernel may reach another device: no remote copies, remote signals or barrier semaphores. Data moves between devices by JAX's collectives and lax.ppermute only.
A program may use at most 64 MiB of HBM per device.

v0:
```python
import jax
import jax.numpy as jnp
from jax import lax
from jax.sharding import PartitionSpec as P

LEAF = 256
RANK = 32
VECS = 4
NEAR_SLOTS = 4
FAR_SLOTS = 6
STEPS = 2
LEAVES_DEV = 1
BASIS = 8
PRECISE = lax.Precision.HIGHEST


def padded_2(block, sides, width):
    for axis, dim in sides:
        count = lax.axis_size(axis)
        forward = [(i, i + 1) for i in range(count - 1)]
        backward = [(target, source) for source, target in forward]
        low = lax.ppermute(
            lax.slice_in_dim(block, block.shape[dim] - width, None, axis=dim), axis, forward
        )
        high = lax.ppermute(lax.slice_in_dim(block, 0, width, axis=dim), axis, backward)
        block = jnp.concatenate([low, block, high], axis=dim)
    return block


def row_products(left_rows, right_rows):
    return jnp.dot(left_rows, right_rows.T, precision=PRECISE)


def near_field(lowered, near_block, near_col, near_count):
    padded = padded_2(lowered, (("clus", 1),), LEAVES_DEV * LEAF)
    leaf_rows = padded.reshape(VECS, 3 * LEAVES_DEV, LEAF)
    first_leaf = (lax.axis_index("clus") - 1) * LEAVES_DEV
    partner_cols = jnp.clip(near_col[0] - first_leaf, 0, 3 * LEAVES_DEV - 1)
    live_count = near_count[0]
    blocks = near_block[0]
    picked = jnp.take(leaf_rows, partner_cols.reshape(-1), axis=1).reshape(
        VECS, LEAVES_DEV, NEAR_SLOTS, LEAF
    )
    slot_ids = lax.broadcasted_iota(jnp.int32, (LEAVES_DEV, NEAR_SLOTS), 1)
    is_live = slot_ids < live_count[:, None]
    picked = jnp.where(is_live[None, :, :, None], picked, jnp.zeros_like(picked))
    result = jnp.einsum("lkpq,vlkq->vlp", blocks, picked, preferred_element_type=jnp.float32)
    return result


def far_field(lowered, far_col, v_basis, u_basis, far_coupling, transfer, top_coupling):
    leaves = lowered.reshape(VECS, LEAVES_DEV, LEAF)
    skeleton = jnp.einsum("lrp,vlp->lvr", v_basis[0], leaves, preferred_element_type=jnp.float32)
    flat_skel = skeleton.reshape(LEAVES_DEV, VECS * RANK)
    wanted = far_col[0].reshape(-1)
    arrived = lax.all_gather(flat_skel, "clus", axis=0, tiled=True)
    arrived_rows = arrived.shape[0]
    matches = (wanted[:, None] == lax.broadcasted_iota(jnp.int32, (1, arrived_rows), 1)).astype(
        jnp.float32
    )
    partners = jnp.dot(matches, arrived, precision=PRECISE)
    partners = partners.reshape(LEAVES_DEV, FAR_SLOTS, VECS, RANK)
    coupled = jnp.einsum("lkqr,lkvr->lvq", far_coupling[0], partners, precision=PRECISE)
    coarse = jnp.einsum("lvr,lrq->vq", skeleton, transfer[0], precision=PRECISE)
    everyone = lax.all_gather(coarse.reshape(1, VECS * RANK), "lvl", axis=0, tiled=True)
    everyone = everyone.reshape(-1, VECS, RANK)
    own_tree = lax.axis_index("lvl")
    couplings = top_coupling[0, 0]
    others = lax.broadcasted_iota(jnp.int32, (couplings.shape[0], 1, 1), 0) != own_tree
    couplings = jnp.where(others, couplings, jnp.zeros_like(couplings))
    upper = jnp.einsum("tqr,tvr->vq", couplings, everyone, precision=PRECISE)
    coupled = coupled + jnp.einsum("lqr,vr->lvq", transfer[0], upper, precision=PRECISE)
    coupled_low = coupled.astype(jnp.bfloat16)
    return jnp.einsum("lvq,lqp->vlp", coupled_low, u_basis[0], preferred_element_type=jnp.float32)


def orthogonalize(window, image_block):
    rows_all = float(lax.axis_size("clus") * lax.axis_size("lvl") * image_block.shape[1])
    metric, projection, square = lax.psum(
        (
            row_products(window, window),
            row_products(window, image_block),
            row_products(image_block, image_block),
        ),
        ("clus", "lvl"),
    )
    metric = metric / rows_all
    projection = projection / rows_all
    square = square / rows_all
    remainder = image_block - jnp.dot(projection.T, window, precision=PRECISE)
    coef_cross = jnp.dot(projection.T, projection, precision=PRECISE)
    weighted = jnp.dot(
        projection.T, jnp.dot(metric, projection, precision=PRECISE), precision=PRECISE
    )
    gram = square - 2.0 * coef_cross + weighted
    lower_factor = jnp.linalg.cholesky(gram)
    inverse = lax.linalg.triangular_solve(
        lower_factor, jnp.eye(VECS, dtype=jnp.float32), left_side=True, lower=True
    )
    new_block = jnp.dot(inverse, remainder, precision=PRECISE)
    return (new_block, jnp.concatenate([projection, lower_factor.T], axis=0))


def local(
    krylov_basis,
    near_block,
    near_col,
    near_count,
    far_col,
    v_basis,
    u_basis,
    far_coupling,
    transfer,
    top_coupling,
):
    row_count = krylov_basis.shape[2]
    window = krylov_basis.reshape(BASIS, row_count)
    current = window[VECS:]
    records = []
    for step_index in range(STEPS):
        lowered = current.astype(jnp.bfloat16)
        near_part = near_field(lowered, near_block, near_col, near_count)
        far_part = far_field(
            lowered, far_col, v_basis, u_basis, far_coupling, transfer, top_coupling
        )
        image_block = (near_part + far_part).reshape(VECS, row_count)
        current, record = orthogonalize(window, image_block)
        records.append(record)
        window = jnp.concatenate([window[VECS:], current], axis=0)
    return (current.reshape(VECS, 1, row_count), jnp.stack(records))


def solution(mesh):
    return jax.shard_map(
        local,
        mesh=mesh,
        in_specs=(
            P(None, "lvl", "clus"),
            P("lvl", "clus", None, None, None),
            P("lvl", "clus", None),
            P("lvl", "clus"),
            P("lvl", "clus", None),
            P("lvl", "clus", None, None),
            P("lvl", "clus", None, None),
            P("lvl", "clus", None, None, None),
            P("lvl", "clus", None, None),
            P("lvl", "clus", None, None, None),
        ),
        out_specs=(P(None, "lvl", "clus"), P()),
        check_vma=False,
    )
```

profile of v0, /device:TPU:10, one launch (start us, length us, event | category | flops | bytes accessed | tf_op | source)
XLA Modules:
  0.0 142.5 jit_solution(8753681522929081642)
XLA Ops:
  0.7 0.7 slice.13
  1.4 2.0 %collective-permute-start.1 = (bf16[4,256]{1,0:T(4,128)(2,1)S(1)}, bf16[4,256]{1,0:T(4,128)(2,1)S(1)}, u32[]{:S(2)}, u32[]{:S(2)}) collective-permute-start(bf16[4,256]{1,0:T(4,128)(2,1)S(1)} %bitcast.165), channel_id=1, source_target_pairs={{4,0},{8,4},{12,8},{16,12},{20,16},{24,20},{28,24},{5,1},{9,5},{13... | collective-permute-start | bytes 6152 | tf_op jit(solution)/shard_map/ppermute | solution.py:25
  3.5 2.4 %collective-permute-start = (bf16[4,256]{1,0:T(4,128)(2,1)S(1)}, bf16[4,256]{1,0:T(4,128)(2,1)S(1)}, u32[]{:S(2)}, u32[]{:S(2)}) collective-permute-start(bf16[4,256]{1,0:T(4,128)(2,1)S(1)} %bitcast.166), channel_id=1, source_target_pairs={{0,4},{4,8},{8,12},{12,16},{16,20},{20,24},{24,28},{1,5},{5,9},{9,... | collective-permute-start | bytes 6152 | tf_op jit(solution)/shard_map/ppermute | solution.py:22
  5.9 0.1 fusion.29
  6.7 0.1 fusion.26
  6.9 9.1 %all-gather = f32[8,1,128]{2,1,0:T(1,128)S(1)} all-gather(f32[1,1,128]{2,1,0:T(1,128)S(1)} %reshape.212), channel_id=1, replica_groups=mesh['clus'=8,'lvl'=4] {'clus'}, dimensions={0}, use_global_device_ids=true | all-gather | bytes 4608 | tf_op jit(solution)/shard_map/all_gather | solution.py:56
  16.0 0.2 fusion.50
  16.2 0.6 copy-done.3
  16.9 0.1 fusion.22
  17.1 8.0 %all-gather.1 = f32[4,1,128]{2,1,0:T(1,128)S(1)} all-gather(f32[1,1,128]{2,1,0:T(1,128)S(1)} %reshape.214), channel_id=1, replica_groups=mesh['clus'=8,'lvl'=4] {'lvl'}, dimensions={0}, use_global_device_ids=true | all-gather | bytes 2560 | tf_op jit(solution)/shard_map/all_gather | solution.py:65
  25.1 0.5 broadcast.208
  25.6 0.7 reduce.10
  26.4 0.2 convolution_bitcast_fusion.9
  26.5 0.3 convolution_bitcast_fusion.8
  26.8 0.2 fusion.6
  27.0 0.6 gather_fusion
  27.6 0.2 convolution_bitcast_fusion.4
  27.9 0.5 copy-done.6
  28.3 0.1 fusion.1
  28.4 0.1 fusion.88
  28.6 0.1 convolution_bitcast_fusion.7
  28.7 41.9 %all-reduce.1 = (f32[4,4]{0,1:T(4,128)S(1)}, f32[8,4]{0,1:T(4,128)S(1)}, f32[8,8]{1,0:T(8,128)S(1)}) all-reduce(f32[4,4]{0,1:T(4,128)S(1)} %fusion.88, f32[8,4]{0,1:T(4,128)S(1)} %convolution_bitcast_fusion.7, f32[8,8]{1,0:T(8,128)S(1)} %fusion.29), channel_id=1, replica_groups=mesh['clus'=8,'lvl'=4] {'clus','lvl'}, use_global_device_ids=true, to_apply=%region_0.2 | all-reduce | flops 112 | bytes 896 | tf_op jit(solution)/shard_map/psum | solution.py:79
  70.6 0.1 convolution_subtract_fusion.1
  70.7 0.1 fusion.5
  70.8 0.1 fusion.47
  71.0 0.1 convolution_add_fusion.2
  71.1 0.1 copy.40
  71.2 0.4 cholesky.44
  71.6 0.6 compare_reduce_fusion.1
  72.3 0.6 fusion.74
  72.9 0.3 custom-call.6
  73.3 0.2 fusion.55
  73.5 0.1 fusion.87
  73.6 1.9 %collective-permute-start.3 = (bf16[4,256]{1,0:T(4,128)(2,1)S(1)}, bf16[4,256]{1,0:T(4,128)(2,1)S(1)}, u32[]{:S(2)}, u32[]{:S(2)}) collective-permute-start(bf16[4,256]{1,0:T(4,128)(2,1)S(1)} %get-tuple-element.23), channel_id=1, source_target_pairs={{4,0},{8,4},{12,8},{16,12},{20,16},{24,20},{28,24},{5,1},{9,5},{13... | collective-permute-start | bytes 6152 | tf_op jit(solution)/shard_map/ppermute | solution.py:25
  75.5 2.4 %collective-permute-start.2 = (bf16[4,256]{1,0:T(4,128)(2,1)S(1)}, bf16[4,256]{1,0:T(4,128)(2,1)S(1)}, u32[]{:S(2)}, u32[]{:S(2)}) collective-permute-start(bf16[4,256]{1,0:T(4,128)(2,1)S(1)} %get-tuple-element.23), channel_id=1, source_target_pairs={{0,4},{4,8},{8,12},{12,16},{16,20},{20,24},{24,28},{1,5},{5,9},{9,... | collective-permute-start | bytes 6152 | tf_op jit(solution)/shard_map/ppermute | solution.py:22
  77.9 0.1 fusion.24
  78.1 0.1 fusion.19
  78.3 8.1 %all-gather.2 = f32[8,1,128]{2,1,0:T(1,128)S(1)} all-gather(f32[1,1,128]{2,1,0:T(1,128)S(1)} %reshape.216), channel_id=1, replica_groups=mesh['clus'=8,'lvl'=4] {'clus'}, dimensions={0}, use_global_device_ids=true | all-gather | bytes 4608 | tf_op jit(solution)/shard_map/all_gather | solution.py:56
  86.4 0.2 fusion.49
  86.7 0.2 convolution_bitcast_fusion.6
  86.9 8.0 %all-gather.3 = f32[4,1,128]{2,1,0:T(1,128)S(1)} all-gather(f32[1,1,128]{2,1,0:T(1,128)S(1)} %reshape.218), channel_id=1, replica_groups=mesh['clus'=8,'lvl'=4] {'lvl'}, dimensions={0}, use_global_device_ids=true | all-gather | bytes 2560 | tf_op jit(solution)/shard_map/all_gather | solution.py:65
  94.9 0.7 reduce.11
  95.6 0.2 convolution_bitcast_fusion.5
  95.9 0.2 fusion.7
  96.0 0.1 fusion.41
  96.2 0.6 gather_fusion.1
  96.8 0.2 convolution_bitcast_fusion.3
  97.0 0.1 fusion.3
  97.1 0.1 fusion.89
  97.3 0.1 fusion.42
  97.4 40.8 %all-reduce = (f32[4,4]{0,1:T(4,128)S(1)}, f32[8,4]{0,1:T(4,128)S(1)}, f32[8,8]{1,0:T(8,128)S(1)}) all-reduce(f32[4,4]{0,1:T(4,128)S(1)} %fusion.89, f32[8,4]{0,1:T(4,128)S(1)} %fusion.42, f32[8,8]{1,0:T(8,128)S(1)} %fusion.41), channel_id=1, replica_groups=mesh['clus'=8,'lvl'=4] {'clus','lvl'}, use_global_device_ids=true, to_apply=%region_5.9 | all-reduce | flops 112 | bytes 896 | tf_op jit(solution)/shard_map/psum | solution.py:79
  138.2 0.1 convolution_subtract_fusion
  138.3 0.1 fusion.4
  138.5 0.1 fusion.45
  138.6 0.1 convolution_add_fusion
  138.7 0.1 copy.45
  138.9 0.4 cholesky.55
  139.3 0.6 compare_reduce_fusion
  139.9 0.6 fusion.73
  140.6 0.3 custom-call.7
  140.9 0.2 fusion.53
  141.1 0.1 convolution_bitcast_fusion.2
  141.2 0.6 copy.47
  141.9 0.6 pad_maximum_fusion.6
  (43 shorter events, 1.0 us)
Async XLA Ops:
  0.6 27.0 %copy-start = (bf16[1,1,4,256,256]{4,3,2,1,0:T(8,128)(2,1)S(1)}, bf16[1,1,4,256,256]{4,3,2,1,0:T(8,128)(2,1)}, u32[]{:S(2)}) copy-start(bf16[1,1,4,256,256]{4,3,2,1,0:T(8,128)(2,1)} %param.16) | copy-start | bytes 1572868
  0.6 5.3 %copy-start.4 = (f32[8,1,256]{2,1,0:T(1,128)S(1)}, f32[8,1,256]{2,1,0:T(1,128)}, u32[]{:S(2)}) copy-start(f32[8,1,256]{2,1,0:T(1,128)} %param.15) | copy-start | bytes 24580
  0.7 5.4 %copy-start.7 = (s32[1,1,4]{2,1,0:T(1,128)S(1)}, s32[1,1,4]{2,1,0:T(1,128)}, u32[]{:S(2)}) copy-start(s32[1,1,4]{2,1,0:T(1,128)} %param.17) | copy-start | bytes 52
  0.7 6.1 %copy-start.5 = (bf16[1,1,32,256]{3,2,1,0:T(8,128)(2,1)S(1)}, bf16[1,1,32,256]{3,2,1,0:T(8,128)(2,1)}, u32[]{:S(2)}) copy-start(bf16[1,1,32,256]{3,2,1,0:T(8,128)(2,1)} %param.20) | copy-start | bytes 49156
  0.7 15.3 %copy-start.8 = (s32[1,1,6]{2,1,0:T(1,128)S(1)}, s32[1,1,6]{2,1,0:T(1,128)}, u32[]{:S(2)}) copy-start(s32[1,1,6]{2,1,0:T(1,128)} %param.19) | copy-start | bytes 76
  1.4 24.9 %copy-start.1 = (f32[1,1,6,32,32]{4,3,2,1,0:T(8,128)S(1)}, f32[1,1,6,32,32]{4,3,2,1,0:T(8,128)}, u32[]{:S(2)}) copy-start(f32[1,1,6,32,32]{4,3,2,1,0:T(8,128)} %param.22) | copy-start | bytes 73732
  1.4 25.5 %collective-permute-start.1 = (bf16[4,256]{1,0:T(4,128)(2,1)S(1)}, bf16[4,256]{1,0:T(4,128)(2,1)S(1)}, u32[]{:S(2)}, u32[]{:S(2)}) collective-permute-start(bf16[4,256]{1,0:T(4,128)(2,1)S(1)} %bitcast.165), channel_id=1, source_target_pairs={{4,0},{8,4},{12,8},{16,12},{20,16},{24,20},{28,24},{5,1},{9,5},{13... | collective-permute-start | bytes 6152 | tf_op jit(solution)/shard_map/ppermute | solution.py:25
  3.5 23.5 %collective-permute-start = (bf16[4,256]{1,0:T(4,128)(2,1)S(1)}, bf16[4,256]{1,0:T(4,128)(2,1)S(1)}, u32[]{:S(2)}, u32[]{:S(2)}) collective-permute-start(bf16[4,256]{1,0:T(4,128)(2,1)S(1)} %bitcast.166), channel_id=1, source_target_pairs={{0,4},{4,8},{8,12},{12,16},{16,20},{20,24},{24,28},{1,5},{5,9},{9,... | collective-permute-start | bytes 6152 | tf_op jit(solution)/shard_map/ppermute | solution.py:22
  16.2 0.7 copy-start.3
  25.6 1.0 copy-start.2
  27.6 0.7 copy-start.6
  73.6 22.6 %collective-permute-start.3 = (bf16[4,256]{1,0:T(4,128)(2,1)S(1)}, bf16[4,256]{1,0:T(4,128)(2,1)S(1)}, u32[]{:S(2)}, u32[]{:S(2)}) collective-permute-start(bf16[4,256]{1,0:T(4,128)(2,1)S(1)} %get-tuple-element.23), channel_id=1, source_target_pairs={{4,0},{8,4},{12,8},{16,12},{20,16},{24,20},{28,24},{5,1},{9,5},{13... | collective-permute-start | bytes 6152 | tf_op jit(solution)/shard_map/ppermute | solution.py:25
  75.5 20.7 %collective-permute-start.2 = (bf16[4,256]{1,0:T(4,128)(2,1)S(1)}, bf16[4,256]{1,0:T(4,128)(2,1)S(1)}, u32[]{:S(2)}, u32[]{:S(2)}) collective-permute-start(bf16[4,256]{1,0:T(4,128)(2,1)S(1)} %get-tuple-element.23), channel_id=1, source_target_pairs={{0,4},{4,8},{8,12},{12,16},{16,20},{20,24},{24,28},{1,5},{5,9},{9,... | collective-permute-start | bytes 6152 | tf_op jit(solution)/shard_map/ppermute | solution.py:22
where the time goes:
time: 143 us
  blocking collectives  116 us (81%)
  starting transfers between devices  8.78 us (6%)
  other arithmetic  6.2 us (4%)
  matrix products  5.25 us (4%)
  local copies, waits for them, and re-layouts  5.02 us (4%)
  between operations  1.52 us (1%)
    psum x2, blocking collectives, orthogonalize(): lax.psum((row_products(window, window), row_products(window, image_block)...  82.6 us
    all_gather x2, blocking collectives, far_field(): arrived = lax.all_gather(flat_skel, 'clus', axis=0, tiled=True)  17.2 us
    all_gather x2, blocking collectives, far_field(): lax.all_gather(coarse.reshape(1, VECS * RANK), 'lvl', axis=0, tiled=True)  15.9 us
    ppermute x2, starting transfers between devices, padded_2(): lax.ppermute(lax.slice_in_dim(block, block.shape[dim] - width, None, axis...  4.81 us
    ppermute x2, starting transfers between devices, padded_2(): lax.ppermute(lax.slice_in_dim(block, 0, width, axis=dim), axis, backward)  3.96 us
  transfers between devices with their start and end apart: 4, of which 0 were waited for; matrix products, arithmetic and copies ran while one was open for 3% of the time, Pallas kernels for 0%

commit v1 on v0

--- a/solution.py
+++ b/solution.py
@@ -2,6 +2,7 @@
 import jax.numpy as jnp
 from jax import lax
 from jax.sharding import PartitionSpec as P
+from jax.lax import psum
 
 LEAF = 256
 RANK = 32
@@ -76,13 +77,16 @@
 
 def orthogonalize(window, image_block):
     rows_all = float(lax.axis_size("clus") * lax.axis_size("lvl") * image_block.shape[1])
-    metric, projection, square = lax.psum(
-        (
-            row_products(window, window),
-            row_products(window, image_block),
-            row_products(image_block, image_block),
+    metric, projection, square = psum(
+        psum(
+            (
+                row_products(window, window),
+                row_products(window, image_block),
+                row_products(image_block, image_block),
+            ),
+            axis_name="lvl",
         ),
-        ("clus", "lvl"),
+        axis_name="clus",
     )
     metric = metric / rows_all
     projection = projection / rows_all

time: 143 us -> 112 us (0.78)
  the two profiles are of different devices: /device:TPU:10 before, /device:TPU:0 now
where the time goes in v1:
time: 112 us
  blocking collectives  84.7 us (76%)
  starting transfers between devices  8.77 us (8%)
  other arithmetic  6.2 us (6%)
  matrix products  5.25 us (5%)
  local copies, waits for them, and re-layouts  5.02 us (4%)
  between operations  1.55 us (1%)
    psum x2, blocking collectives, orthogonalize(): psum(psum((row_products(window, window), row_products(window, image_block...  27.8 us
    all_gather x2, blocking collectives, far_field(): arrived = lax.all_gather(flat_skel, 'clus', axis=0, tiled=True)  22.8 us
    psum x2, blocking collectives, orthogonalize(): psum((row_products(window, window), row_products(window, image_block), ro...  18.2 us
    all_gather x2, blocking collectives, far_field(): lax.all_gather(coarse.reshape(1, VECS * RANK), 'lvl', axis=0, tiled=True)  15.9 us
    ppermute x2, starting transfers between devices, padded_2(): lax.ppermute(lax.slice_in_dim(block, block.shape[dim] - width, None, axis...  6.06 us
    ppermute x2, starting transfers between devices, padded_2(): lax.ppermute(lax.slice_in_dim(block, 0, width, axis=dim), axis, backward)  2.71 us
  transfers between devices with their start and end apart: 4, of which 0 were waited for; matrix products, arithmetic and copies ran while one was open for 4% of the time, Pallas kernels for 0%

profile of v1, /device:TPU:0, one launch (start us, length us, event | category | flops | bytes accessed | tf_op | source)
XLA Modules:
  0.0 111.5 jit_solution(11979445094377019396)
XLA Ops:
  0.7 0.7 slice.13
  1.4 1.4 %collective-permute-start.1 = (bf16[4,256]{1,0:T(4,128)(2,1)S(1)}, bf16[4,256]{1,0:T(4,128)(2,1)S(1)}, u32[]{:S(2)}, u32[]{:S(2)}) collective-permute-start(bf16[4,256]{1,0:T(4,128)(2,1)S(1)} %bitcast.165), channel_id=1, source_target_pairs={{4,0},{8,4},{12,8},{16,12},{20,16},{24,20},{28,24},{5,1},{9,5},{13... | collective-permute-start | bytes 6152 | tf_op jit(solution)/shard_map/ppermute | solution.py:26
  2.9 3.0 %collective-permute-start = (bf16[4,256]{1,0:T(4,128)(2,1)S(1)}, bf16[4,256]{1,0:T(4,128)(2,1)S(1)}, u32[]{:S(2)}, u32[]{:S(2)}) collective-permute-start(bf16[4,256]{1,0:T(4,128)(2,1)S(1)} %bitcast.166), channel_id=1, source_target_pairs={{0,4},{4,8},{8,12},{12,16},{16,20},{20,24},{24,28},{1,5},{5,9},{9,... | collective-permute-start | bytes 6152 | tf_op jit(solution)/shard_map/ppermute | solution.py:23
  5.9 0.1 fusion.29
  6.7 0.1 fusion.26
  6.9 13.5 %all-gather = f32[8,1,128]{2,1,0:T(1,128)S(1)} all-gather(f32[1,1,128]{2,1,0:T(1,128)S(1)} %reshape.212), channel_id=1, replica_groups=mesh['clus'=8,'lvl'=4] {'clus'}, dimensions={0}, use_global_device_ids=true | all-gather | bytes 4608 | tf_op jit(solution)/shard_map/all_gather | solution.py:57
  20.4 0.2 fusion.50
  20.6 0.6 copy-done.3
  21.3 0.1 fusion.22
  21.5 8.0 %all-gather.1 = f32[4,1,128]{2,1,0:T(1,128)S(1)} all-gather(f32[1,1,128]{2,1,0:T(1,128)S(1)} %reshape.214), channel_id=1, replica_groups=mesh['clus'=8,'lvl'=4] {'lvl'}, dimensions={0}, use_global_device_ids=true | all-gather | bytes 2560 | tf_op jit(solution)/shard_map/all_gather | solution.py:66
  29.5 0.5 broadcast.208
  30.0 0.7 reduce.10
  30.8 0.2 convolution_bitcast_fusion.9
  30.9 0.3 convolution_bitcast_fusion.8
  31.2 0.2 fusion.6
  31.4 0.6 gather_fusion
  32.0 0.2 convolution_bitcast_fusion.4
  32.3 0.5 copy-done.6
  32.7 0.1 fusion.1
  32.8 0.1 fusion.88
  33.0 0.1 convolution_bitcast_fusion.7
  33.1 9.1 %all-reduce.3 = (f32[4,4]{0,1:T(4,128)S(1)}, f32[8,4]{0,1:T(4,128)S(1)}, f32[8,8]{1,0:T(8,128)S(1)}) all-reduce(f32[4,4]{0,1:T(4,128)S(1)} %fusion.88, f32[8,4]{0,1:T(4,128)S(1)} %convolution_bitcast_fusion.7, f32[8,8]{1,0:T(8,128)S(1)} %fusion.29), channel_id=1, replica_groups=mesh['clus'=8,'lvl'=4] {'lvl'}, use_global_device_ids=true, to_apply=%region_0.2 | all-reduce | flops 112 | bytes 896 | tf_op jit(solution)/shard_map/psum | solution.py:81
  42.2 13.9 %all-reduce.1 = (f32[4,4]{0,1:T(4,128)S(1)}, f32[8,4]{0,1:T(4,128)S(1)}, f32[8,8]{1,0:T(8,128)S(1)}) all-reduce(f32[4,4]{0,1:T(4,128)S(1)} %get-tuple-element.20, f32[8,4]{0,1:T(4,128)S(1)} %get-tuple-element.21, f32[8,8]{1,0:T(8,128)S(1)} %get-tuple-element.22), channel_id=1, replica_groups=mesh['clus'=8,'lvl'=4] {'clus'}, use_global_device_ids=true, to_apply=%region_1.3 | all-reduce | flops 112 | bytes 896 | tf_op jit(solution)/shard_map/psum | solution.py:80
  56.1 0.1 convolution_subtract_fusion.1
  56.2 0.1 fusion.5
  56.4 0.1 fusion.47
  56.5 0.1 convolution_add_fusion.2
  56.8 0.4 cholesky.44
  57.2 0.6 compare_reduce_fusion.1
  57.8 0.6 fusion.74
  58.5 0.3 custom-call.6
  58.8 0.2 fusion.55
  59.0 0.1 fusion.87
  59.2 1.3 %collective-permute-start.3 = (bf16[4,256]{1,0:T(4,128)(2,1)S(1)}, bf16[4,256]{1,0:T(4,128)(2,1)S(1)}, u32[]{:S(2)}, u32[]{:S(2)}) collective-permute-start(bf16[4,256]{1,0:T(4,128)(2,1)S(1)} %get-tuple-element.29), channel_id=1, source_target_pairs={{4,0},{8,4},{12,8},{16,12},{20,16},{24,20},{28,24},{5,1},{9,5},{13... | collective-permute-start | bytes 6152 | tf_op jit(solution)/shard_map/ppermute | solution.py:26
  60.5 3.0 %collective-permute-start.2 = (bf16[4,256]{1,0:T(4,128)(2,1)S(1)}, bf16[4,256]{1,0:T(4,128)(2,1)S(1)}, u32[]{:S(2)}, u32[]{:S(2)}) collective-permute-start(bf16[4,256]{1,0:T(4,128)(2,1)S(1)} %get-tuple-element.29), channel_id=1, source_target_pairs={{0,4},{4,8},{8,12},{12,16},{16,20},{20,24},{24,28},{1,5},{5,9},{9,... | collective-permute-start | bytes 6152 | tf_op jit(solution)/shard_map/ppermute | solution.py:23
  63.5 0.1 fusion.24
  63.7 0.1 fusion.19
  63.8 9.4 %all-gather.2 = f32[8,1,128]{2,1,0:T(1,128)S(1)} all-gather(f32[1,1,128]{2,1,0:T(1,128)S(1)} %reshape.216), channel_id=1, replica_groups=mesh['clus'=8,'lvl'=4] {'clus'}, dimensions={0}, use_global_device_ids=true | all-gather | bytes 4608 | tf_op jit(solution)/shard_map/all_gather | solution.py:57
  73.2 0.2 fusion.49
  73.5 0.2 convolution_bitcast_fusion.6
  73.7 7.9 %all-gather.3 = f32[4,1,128]{2,1,0:T(1,128)S(1)} all-gather(f32[1,1,128]{2,1,0:T(1,128)S(1)} %reshape.218), channel_id=1, replica_groups=mesh['clus'=8,'lvl'=4] {'lvl'}, dimensions={0}, use_global_device_ids=true | all-gather | bytes 2560 | tf_op jit(solution)/shard_map/all_gather | solution.py:66
  81.6 0.7 reduce.11
  82.4 0.2 convolution_bitcast_fusion.5
  82.6 0.2 fusion.7
  82.8 0.1 fusion.41
  83.0 0.6 gather_fusion.1
  83.5 0.2 convolution_bitcast_fusion.3
  83.8 0.1 fusion.3
  83.9 0.1 fusion.89
  84.1 0.1 fusion.42
  84.2 9.1 %all-reduce.2 = (f32[4,4]{0,1:T(4,128)S(1)}, f32[8,4]{0,1:T(4,128)S(1)}, f32[8,8]{1,0:T(8,128)S(1)}) all-reduce(f32[4,4]{0,1:T(4,128)S(1)} %fusion.89, f32[8,4]{0,1:T(4,128)S(1)} %fusion.42, f32[8,8]{1,0:T(8,128)S(1)} %fusion.41), channel_id=1, replica_groups=mesh['clus'=8,'lvl'=4] {'lvl'}, use_global_device_ids=true, to_apply=%region_8.12 | all-reduce | flops 112 | bytes 896 | tf_op jit(solution)/shard_map/psum | solution.py:81
  93.3 13.9 %all-reduce = (f32[4,4]{0,1:T(4,128)S(1)}, f32[8,4]{0,1:T(4,128)S(1)}, f32[8,8]{1,0:T(8,128)S(1)}) all-reduce(f32[4,4]{0,1:T(4,128)S(1)} %get-tuple-element.17, f32[8,4]{0,1:T(4,128)S(1)} %get-tuple-element.18, f32[8,8]{1,0:T(8,128)S(1)} %get-tuple-element.19), channel_id=1, replica_groups=mesh['clus'=8,'lvl'=4] {'clus'}, use_global_device_ids=true, to_apply=%region_9.13 | all-reduce | flops 112 | bytes 896 | tf_op jit(solution)/shard_map/psum | solution.py:80
  107.2 0.1 convolution_subtract_fusion
  107.3 0.1 fusion.4
  107.5 0.1 fusion.45
  107.6 0.1 convolution_add_fusion
  107.9 0.4 cholesky.55
  108.3 0.6 compare_reduce_fusion
  108.9 0.6 fusion.73
  109.6 0.3 custom-call.7
  109.9 0.2 fusion.53
  110.1 0.1 convolution_bitcast_fusion.2
  110.2 0.6 copy.47
  110.9 0.6 pad_maximum_fusion.6
  (45 shorter events, 1.2 us)
Async XLA Ops:
  0.6 31.4 %copy-start = (bf16[1,1,4,256,256]{4,3,2,1,0:T(8,128)(2,1)S(1)}, bf16[1,1,4,256,256]{4,3,2,1,0:T(8,128)(2,1)}, u32[]{:S(2)}) copy-start(bf16[1,1,4,256,256]{4,3,2,1,0:T(8,128)(2,1)} %param.16) | copy-start | bytes 1572868
  0.6 5.2 %copy-start.4 = (f32[8,1,256]{2,1,0:T(1,128)S(1)}, f32[8,1,256]{2,1,0:T(1,128)}, u32[]{:S(2)}) copy-start(f32[8,1,256]{2,1,0:T(1,128)} %param.15) | copy-start | bytes 24580
  0.7 5.4 %copy-start.7 = (s32[1,1,4]{2,1,0:T(1,128)S(1)}, s32[1,1,4]{2,1,0:T(1,128)}, u32[]{:S(2)}) copy-start(s32[1,1,4]{2,1,0:T(1,128)} %param.17) | copy-start | bytes 52
  0.7 6.0 %copy-start.5 = (bf16[1,1,32,256]{3,2,1,0:T(8,128)(2,1)S(1)}, bf16[1,1,32,256]{3,2,1,0:T(8,128)(2,1)}, u32[]{:S(2)}) copy-start(bf16[1,1,32,256]{3,2,1,0:T(8,128)(2,1)} %param.20) | copy-start | bytes 49156
  0.7 19.7 %copy-start.8 = (s32[1,1,6]{2,1,0:T(1,128)S(1)}, s32[1,1,6]{2,1,0:T(1,128)}, u32[]{:S(2)}) copy-start(s32[1,1,6]{2,1,0:T(1,128)} %param.19) | copy-start | bytes 76
  1.4 29.3 %copy-start.1 = (f32[1,1,6,32,32]{4,3,2,1,0:T(8,128)S(1)}, f32[1,1,6,32,32]{4,3,2,1,0:T(8,128)}, u32[]{:S(2)}) copy-start(f32[1,1,6,32,32]{4,3,2,1,0:T(8,128)} %param.22) | copy-start | bytes 73732
  1.4 29.9 %collective-permute-start.1 = (bf16[4,256]{1,0:T(4,128)(2,1)S(1)}, bf16[4,256]{1,0:T(4,128)(2,1)S(1)}, u32[]{:S(2)}, u32[]{:S(2)}) collective-permute-start(bf16[4,256]{1,0:T(4,128)(2,1)S(1)} %bitcast.165), channel_id=1, source_target_pairs={{4,0},{8,4},{12,8},{16,12},{20,16},{24,20},{28,24},{5,1},{9,5},{13... | collective-permute-start | bytes 6152 | tf_op jit(solution)/shard_map/ppermute | solution.py:26
  2.9 28.5 %collective-permute-start = (bf16[4,256]{1,0:T(4,128)(2,1)S(1)}, bf16[4,256]{1,0:T(4,128)(2,1)S(1)}, u32[]{:S(2)}, u32[]{:S(2)}) collective-permute-start(bf16[4,256]{1,0:T(4,128)(2,1)S(1)} %bitcast.166), channel_id=1, source_target_pairs={{0,4},{4,8},{8,12},{12,16},{16,20},{20,24},{24,28},{1,5},{5,9},{9,... | collective-permute-start | bytes 6152 | tf_op jit(solution)/shard_map/ppermute | solution.py:23
  20.6 0.7 copy-start.3
  30.0 1.0 copy-start.2
  32.0 0.7 copy-start.6
  59.2 23.8 %collective-permute-start.3 = (bf16[4,256]{1,0:T(4,128)(2,1)S(1)}, bf16[4,256]{1,0:T(4,128)(2,1)S(1)}, u32[]{:S(2)}, u32[]{:S(2)}) collective-permute-start(bf16[4,256]{1,0:T(4,128)(2,1)S(1)} %get-tuple-element.29), channel_id=1, source_target_pairs={{4,0},{8,4},{12,8},{16,12},{20,16},{24,20},{28,24},{5,1},{9,5},{13... | collective-permute-start | bytes 6152 | tf_op jit(solution)/shard_map/ppermute | solution.py:26
  60.5 22.5 %collective-permute-start.2 = (bf16[4,256]{1,0:T(4,128)(2,1)S(1)}, bf16[4,256]{1,0:T(4,128)(2,1)S(1)}, u32[]{:S(2)}, u32[]{:S(2)}) collective-permute-start(bf16[4,256]{1,0:T(4,128)(2,1)S(1)} %get-tuple-element.29), channel_id=1, source_target_pairs={{0,4},{4,8},{8,12},{12,16},{16,20},{20,24},{24,28},{1,5},{5,9},{9,... | collective-permute-start | bytes 6152 | tf_op jit(solution)/shard_map/ppermute | solution.py:23
